TPU v7x, 128 devices: a whole 4x4x4 slice. The times are simulated.
128 devices in a mesh: col: 32 (over y, x, core), row: 4 (over z).
Axes of the slice: x: 4, y: 4, z: 4, core: 2. Of those that a mesh axis runs over, the one named last changes fastest.
Arguments:
- sources_field: float32 [2, 31744, 128], P(None, ('col', 'row')), may hold values from -6 to 6
- data: float32 [2, 52224, 128], P(None, ('col', 'row')), may hold values from -6 to 6
- left_basis: float32 [2, 32, 52224, 128], P(None, None, ('col', 'row')), may hold values from -0.09375 to 0.09375
- right_basis: float32 [2, 32, 31744, 128], P(None, None, ('col', 'row')), may hold values from -0.1875 to 0.1875
- ranks: int32 [32, 32], replicated, may hold values from 32 to 128, as said below
Outputs:
- residual: float32 [2, 52224, 128], P(None, ('col', 'row'))
- gradient: float32 [2, 31744, 128], P(None, ('col', 'row'))
Inputs may be any that keep to these rules, and one draw needn't show every extreme that they name: `ranks`: every rank is a multiple of 32.
All inputs are finite; a program needn't handle non-finite values.
Results may differ from a plain program's by a relative error of at most 0.000059.
Values sent between devices are 32-bit elements; how exact they have to be, the bound alone decides.
A program may use at most 128 MiB of HBM per device.

v0:
```python
import jax
import jax.numpy as jnp
from jax import lax
from jax.sharding import PartitionSpec as P


def contract(form, left, right):
    return jnp.einsum(
        form, left, right, precision=lax.Precision.HIGHEST, preferred_element_type=jnp.float32
    )


def on_device(sources_field, data, left_basis, right_basis, ranks):
    column = lax.axis_index("col")
    kmax = right_basis.shape[-1]
    levels = jnp.arange(kmax, dtype=jnp.int32)
    rank_column = lax.dynamic_slice_in_dim(ranks, column, 1, 1)[:, 0]
    rank_stripe = lax.dynamic_slice_in_dim(ranks, column, 1, 0)[0]
    keep_right = (levels[None, :] < rank_column[:, None]).astype(jnp.float32)[:, :, None]
    keep_left = (levels[None, :] < rank_stripe[:, None]).astype(jnp.float32)[:, :, None]
    right_real, right_imag = (right_basis[0], right_basis[1])
    left_real, left_imag = (left_basis[0], left_basis[1])
    field_real, field_imag = (sources_field[0], sources_field[1])
    coeff_real = contract("ink,ns->iks", right_real, field_real) + contract(
        "ink,ns->iks", right_imag, field_imag
    )
    coeff_imag = contract("ink,ns->iks", right_real, field_imag) - contract(
        "ink,ns->iks", right_imag, field_real
    )
    partial_coeff = jnp.stack([coeff_real * keep_right, coeff_imag * keep_right])
    summed = lax.psum(partial_coeff, "row")
    coeff = lax.all_to_all(summed, "col", split_axis=1, concat_axis=1, tiled=True)
    pred_real = contract("jmk,jks->ms", left_real, coeff[0]) - contract(
        "jmk,jks->ms", left_imag, coeff[1]
    )
    pred_imag = contract("jmk,jks->ms", left_real, coeff[1]) + contract(
        "jmk,jks->ms", left_imag, coeff[0]
    )
    residual = jnp.stack([pred_real, pred_imag]) - data
    resid_real, resid_imag = (residual[0], residual[1])
    back_real = contract("jmk,ms->jks", left_real, resid_real) + contract(
        "jmk,ms->jks", left_imag, resid_imag
    )
    back_imag = contract("jmk,ms->jks", left_real, resid_imag) - contract(
        "jmk,ms->jks", left_imag, resid_real
    )
    partial_back = jnp.stack([back_real * keep_left, back_imag * keep_left])
    back_sum = lax.psum(partial_back, "row")
    adjoint = lax.all_to_all(back_sum, "col", split_axis=1, concat_axis=1, tiled=True)
    grad_real = contract("ink,iks->ns", right_real, adjoint[0]) - contract(
        "ink,iks->ns", right_imag, adjoint[1]
    )
    grad_imag = contract("ink,iks->ns", right_real, adjoint[1]) + contract(
        "ink,iks->ns", right_imag, adjoint[0]
    )
    gradient = jnp.stack([grad_real, grad_imag])
    return (residual, gradient)


def solution(mesh):
    placed = (
        P(None, ("col", "row"), None),
        P(None, ("col", "row"), None),
        P(None, None, ("col", "row"), None),
        P(None, None, ("col", "row"), None),
        P(),
    )
    return jax.shard_map(
        on_device,
        mesh=mesh,
        in_specs=placed,
        out_specs=(P(None, ("col", "row"), None), P(None, ("col", "row"), None)),
        check_vma=False,
    )
```

profile of v0, /device:TPU:0, one launch (start us, length us, event | category | flops | bytes accessed | tf_op | source)
XLA Modules:
  0.0 431.8 jit_solution(936456935435610461)
XLA Ops:
  7.2 0.0 all-reduce.3.cloned.1.call-start
  7.2 10.2 %fusion.28 = f32[32,128,128]{2,1,0:T(8,128)} fusion(f32[2,32,248,128]{3,2,1,0:T(8,128)} %param.8, f32[2,248,128]{2,1,0:T(8,128)} %param.5), kind=kOutput, calls=%fused_computation.30 | convolution fusion | flops 1560281088 | bytes 6287360 | tf_op jit(solution)/shard_map/ink,ns->iks/dot_general | solution.py:8
  17.5 8.6 %fusion.30 = f32[32,128,128]{2,1,0:T(8,128)S(1)} fusion(f32[2,32,248,128]{3,2,1,0:T(8,128)} %param.8, f32[2,248,128]{2,1,0:T(8,128)S(1)} %copy-done.3), kind=kOutput, calls=%fused_computation.32 | convolution fusion | flops 1560281088 | bytes 6287360 | tf_op jit(solution)/shard_map/ink,ns->iks/dot_general | solution.py:8
  26.1 0.2 dynamic-slice_reduce_fusion
  26.3 0.1 fusion.112
  26.4 10.0 %multiply_bitcast_fusion.2 = f32[1,32,128,128]{3,2,1,0:T(8,128)S(1)} fusion(f32[32,128,128]{2,1,0:T(8,128)} %fusion.28, f32[2,32,248,128]{3,2,1,0:T(8,128)} %param.8, f32[32,128]{1,0:T(8,128)S(1)} %fusion.112, f32[2,248,128]{2,1,0:T(8,128)S(1)} %copy-done.3), kind=kOutput, calls=%fused_computation.56 | convolution fusion | flops 1561329664 | bytes 8400896 | tf_op jit(solution)/shard_map/ink,ns->iks/dot_general | solution.py:8
  36.4 9.2 %multiply_bitcast_fusion.3 = f32[1,32,128,128]{3,2,1,0:T(8,128)S(1)} fusion(f32[32,128,128]{2,1,0:T(8,128)S(1)} %fusion.30, f32[2,32,248,128]{3,2,1,0:T(8,128)} %param.8, f32[32,128]{1,0:T(8,128)S(1)} %fusion.112, f32[2,248,128]{2,1,0:T(8,128)S(1)} %copy-done.3), kind=kOutput, calls=%fused_computation.57 | convolution fusion | flops 1561329664 | bytes 8400896 | tf_op jit(solution)/shard_map/ink,ns->iks/dot_general | solution.py:8
  45.6 2.3 pad_maximum_fusion
  47.9 95.7 %all-reduce.3.cloned.1.call-done = f32[2,32,128,128]{3,2,1,0:T(8,128)} async-done(((f32[2,32,128,128]{3,2,1,0:T(8,128)}), f32[2,32,128,128]{3,2,1,0:T(8,128)}) %all-reduce.3.cloned.1.call-update) | async-done | bytes 4194320 | tf_op jit(solution)/shard_map/psum | solution.py:31
  143.6 4.7 %copy.15 = f32[2,32,128,128]{3,2,0,1:T(8,128)} copy(f32[2,32,128,128]{3,2,1,0:T(8,128)} %all-reduce.3.cloned.1.call-done) | data formatting | bytes 8388608 | tf_op jit(solution)/shard_map/psum | solution.py:31
  148.2 7.2 %all-to-all-start = ((f32[2,32,128,128]{3,2,0,1:T(8,128)}), f32[2,32,128,128]{3,2,0,1:T(8,128)}, u32[]{:S(2)}, u32[]{:S(2)}) async-start(f32[2,32,128,128]{3,2,0,1:T(8,128)} %copy.15), calls=%async_computation | async-start | bytes 8388608 | tf_op jit(solution)/shard_map/all_to_all | solution.py:32
  155.5 0.0 all-reduce.5.cloned.1.call-start
  155.5 0.1 fusion.113
  155.6 53.8 %all-to-all-done = f32[2,32,128,128]{3,2,0,1:T(8,128)} async-done(((f32[2,32,128,128]{3,2,0,1:T(8,128)}), f32[2,32,128,128]{3,2,0,1:T(8,128)}, u32[]{:S(2)}, u32[]{:S(2)}) %all-to-all-start) | async-done | bytes 4194336 | tf_op jit(solution)/shard_map/all_to_all | solution.py:32
  209.4 8.7 %fusion.59 = f32[128,408]{0,1:T(8,128)S(1)} fusion(f32[2,32,408,128]{3,2,1,0:T(8,128)} %param.7, f32[2,32,128,128]{3,2,0,1:T(8,128)} %all-to-all-done), kind=kOutput, calls=%fused_computation.59 | convolution fusion | flops 2566914048 | bytes 8990720 | tf_op jit(solution)/shard_map/jmk,jks->ms/dot_general | solution.py:8
  218.1 8.7 %fusion.56 = f32[128,408]{0,1:T(8,128)S(1)} fusion(f32[2,32,408,128]{3,2,1,0:T(8,128)} %param.7, f32[2,32,128,128]{3,2,0,1:T(8,128)} %all-to-all-done), kind=kOutput, calls=%fused_computation.58 | convolution fusion | flops 2566914048 | bytes 8990720 | tf_op jit(solution)/shard_map/jmk,jks->ms/dot_general | solution.py:8
  226.9 8.9 %fusion.71 = f32[1,408,128]{2,1,0:T(8,128)S(1)} fusion(f32[128,408]{0,1:T(8,128)S(1)} %fusion.59, f32[2,32,408,128]{3,2,1,0:T(8,128)} %param.7, f32[2,32,128,128]{3,2,0,1:T(8,128)} %all-to-all-done), kind=kOutput, calls=%fused_computation.63 | convolution fusion | flops 2566966272 | bytes 9199616 | tf_op jit(solution)/shard_map/jmk,jks->ms/dot_general | solution.py:8
  235.9 7.0 %fusion.77 = f32[1,408,128]{2,1,0:T(8,128)S(1)} fusion(f32[128,408]{0,1:T(8,128)S(1)} %fusion.56, f32[2,32,408,128]{3,2,1,0:T(8,128)S(1)} %bitcast.217, f32[2,32,128,128]{3,2,0,1:T(8,128)} %all-to-all-done), kind=kOutput, calls=%fused_computation.65 | convolution fusion | flops 2566966272 | bytes 9199616 | tf_op jit(solution)/shard_map/jmk,jks->ms/dot_general | solution.py:8
  242.9 0.1 maximum_subtract_fusion
  243.0 3.9 fusion
  246.9 4.3 %fusion.2 = f32[128,32,128]{2,0,1:T(8,128)S(1)} fusion(f32[2,32,408,128]{3,2,1,0:T(8,128)S(1)} %bitcast.217, f32[2,408,128]{2,1,0:T(8,128)S(1)} %maximum_subtract_fusion), kind=kOutput, calls=%fused_computation.2 | convolution fusion | flops 2566914048 | bytes 8990720 | tf_op jit(solution)/shard_map/jmk,ms->jks/dot_general | solution.py:8
  251.2 4.0 multiply_bitcast_fusion
  255.2 4.0 multiply_bitcast_fusion.1
  259.2 2.5 pad_maximum_fusion.1
  261.7 88.3 %all-reduce.5.cloned.1.call-done = f32[2,32,128,128]{2,3,1,0:T(8,128)} async-done(((f32[2,32,128,128]{2,3,1,0:T(8,128)}), f32[2,32,128,128]{2,3,1,0:T(8,128)}) %all-reduce.5.cloned.1.call-update) | async-done | bytes 4194320 | tf_op jit(solution)/shard_map/psum | solution.py:48
  350.0 2.6 copy.18
  352.6 58.1 %all_to_all.10 = f32[2,32,128,128]{2,3,0,1:T(8,128)S(1)} all-to-all(f32[2,32,128,128]{2,3,0,1:T(8,128)S(1)} %copy.18), channel_id=1, replica_groups=mesh['col'=32,'row'=4] {'col'}, dimensions={1} | all-to-all | bytes 8388608 | tf_op jit(solution)/shard_map/all_to_all | solution.py:49
  410.7 3.3 fusion.83
  414.1 3.3 fusion.80
  417.4 3.4 fusion.95
  420.8 3.3 fusion.101
  424.1 0.7 pad_maximum_fusion.2
  (27 shorter events, 0.1 us)
Async XLA Ops:
  7.2 19.0 %copy-start = (s32[32,32]{1,0:T(8,128)S(1)}, s32[32,32]{1,0:T(8,128)}, u32[]{:S(2)}) copy-start(s32[32,32]{1,0:T(8,128)} %param.9) | copy-start | bytes 12292
  7.2 10.3 %copy-start.3 = (f32[2,248,128]{2,1,0:T(8,128)S(1)}, f32[2,248,128]{2,1,0:T(8,128)}, u32[]{:S(2)}) copy-start(f32[2,248,128]{2,1,0:T(8,128)} %param.5) | copy-start | bytes 761860
  7.2 136.4 %all-reduce.3.cloned.1.call-start = ((), (), s32[]{:S(2)}) async-start(), calls=%async_computation.2 | async-start | bytes 8388608 | tf_op jit(solution)/shard_map/psum | solution.py:31
  148.2 61.2 %all-to-all-start = ((f32[2,32,128,128]{3,2,0,1:T(8,128)}), f32[2,32,128,128]{3,2,0,1:T(8,128)}, u32[]{:S(2)}, u32[]{:S(2)}) async-start(f32[2,32,128,128]{3,2,0,1:T(8,128)} %copy.15), calls=%async_computation | async-start | bytes 8388608 | tf_op jit(solution)/shard_map/all_to_all | solution.py:32
  155.5 194.6 %all-reduce.5.cloned.1.call-start = ((), (), s32[]{:S(2)}) async-start(), calls=%async_computation.3 | async-start | bytes 8388608 | tf_op jit(solution)/shard_map/psum | solution.py:48
  209.4 26.4 %slice-start = ((s8[13369344]{0:T(1024)(128)(4,1)}), s8[4194304]{0:T(1024)(128)(4,1)S(1)}, s32[]{:S(2)}) async-start(s8[13369344]{0:T(1024)(128)(4,1)} %bitcast.216), calls=%async_computation.4 | async-start | bytes 8388608
  209.4 26.4 %slice-start.1 = ((s8[13369344]{0:T(1024)(128)(4,1)}), s8[4194304]{0:T(1024)(128)(4,1)S(1)}, s32[]{:S(2)}) async-start(s8[13369344]{0:T(1024)(128)(4,1)} %bitcast.216), calls=%async_computation.5 | async-start | bytes 8388608
  218.1 17.7 %slice-start.2 = ((s8[13369344]{0:T(1024)(128)(4,1)}), s8[4194304]{0:T(1024)(128)(4,1)S(1)}, s32[]{:S(2)}) async-start(s8[13369344]{0:T(1024)(128)(4,1)} %bitcast.216), calls=%async_computation.6 | async-start | bytes 8388608
  226.9 8.9 %slice-start.3 = ((s8[13369344]{0:T(1024)(128)(4,1)}), s8[786432]{0:T(1024)(128)(4,1)S(1)}, s32[]{:S(2)}) async-start(s8[13369344]{0:T(1024)(128)(4,1)} %bitcast.216), calls=%async_computation.7 | async-start | bytes 1572864
  235.8 7.0 %copy-start.4 = (f32[2,408,128]{2,1,0:T(8,128)S(1)}, f32[2,408,128]{2,1,0:T(8,128)}, u32[]{:S(2)}) copy-start(f32[2,408,128]{2,1,0:T(8,128)} %param.6) | copy-start | bytes 1253380
  243.0 12.3 %copy-start.2 = (f32[2,408,128]{2,1,0:T(8,128)}, f32[2,408,128]{2,1,0:T(8,128)S(1)}, u32[]{:S(2)}) copy-start(f32[2,408,128]{2,1,0:T(8,128)S(1)} %maximum_subtract_fusion) | copy-start | bytes 1253380
  350.0 60.7 %slice-start.4 = ((s8[8126464]{0:T(1024)(128)(4,1)}), s8[3932160]{0:T(1024)(128)(4,1)S(1)}, s32[]{:S(2)}) async-start(s8[8126464]{0:T(1024)(128)(4,1)} %bitcast.218), calls=%async_computation.8 | async-start | bytes 7864320
  352.6 58.1 %slice-start.5 = ((s8[8126464]{0:T(1024)(128)(4,1)}), s8[4194304]{0:T(1024)(128)(4,1)S(1)}, s32[]{:S(2)}) async-start(s8[8126464]{0:T(1024)(128)(4,1)} %bitcast.218), calls=%async_computation.9 | async-start | bytes 8388608
  417.4 7.4 %copy-start.1 = (s32[32,32]{1,0:T(8,128)S(1)}, s32[32,32]{1,0:T(8,128)}, u32[]{:S(2)}) copy-start(s32[32,32]{1,0:T(8,128)} %param.9) | copy-start | bytes 12292
Sparse Core Ops, SparseCore 0:
  48.0 95.5 all-reduce.2
  261.8 88.1 all-reduce.4
where the time goes:
time: 438 us; the launch traced here: 432 us
  waiting for transfers between devices  238 us (54%)
  matrix products  101 us (23%)
  blocking collectives  58.1 us (13%)
  between operations  14.5 us (3%)
  local copies, waits for them, and re-layouts  7.53 us (2%)
  starting transfers between devices  7.3 us (2%)
  other arithmetic  5.68 us (1%)
    dot_general x16, matrix products, contract(): jnp.einsum(form, left, right, precision=lax.Precision.HIGHEST, preferred_...  101 us
    psum x1, waiting for transfers between devices, on_device(): summed = lax.psum(partial_coeff, 'row')  95.7 us
    psum x1, waiting for transfers between devices, on_device(): back_sum = lax.psum(partial_back, 'row')  88.3 us
    all_to_all x1, blocking collectives, on_device(): lax.all_to_all(back_sum, 'col', split_axis=1, concat_axis=1, tiled=True)  58.1 us
    all_to_all x1, waiting for transfers between devices, on_device(): lax.all_to_all(summed, 'col', split_axis=1, concat_axis=1, tiled=True)  53.8 us
  transfers between devices with their start and end apart: 3, of which 3 were waited for; matrix products, arithmetic and copies ran while one was open for 0% of the time, Pallas kernels for 0%

commit v1 on v0

v1 whole, which is shorter than its diff:
```python
import functools

import jax
import jax.numpy as jnp
from jax import lax
from jax.experimental import pallas as pl
from jax.experimental.pallas import tpu as pltpu
from jax.sharding import PartitionSpec as P

MESH = pl.DeviceIdType.MESH
F32 = jnp.float32
BF16 = jnp.bfloat16
GROUP = 4


def halves(a):
    hi = a.astype(BF16)
    return hi, (a - hi.astype(F32)).astype(BF16)


def dot3(a, b, contract):
    def dot(x, y):
        return lax.dot_general(x, y, (contract, ((), ())), preferred_element_type=F32)

    (ah, al), (bh, bl) = a, b
    return dot(ah, bh) + (dot(ah, bl) + dot(al, bh))


def kernel(
    tiles, group, ranks, x_any, d_any, u_any, v_any, res_any, grad_any,
    x, d, u, v, part, r1, r2, z, xt, rt, acc_u, acc_v, grad,
    x_sem, d_sem, v_sem, u_sem, out_sem, self_sem,
    rs1_send, rs2_send, a2a_send, ag1_send, ag2_send,
    rs1_recv, rs2_recv, a2a_recv, ag1_recv, ag2_recv,
):
    c = lax.axis_index("col")
    r = lax.axis_index("row")
    s = part.shape[-2]
    quarter = s // 4
    groups = tiles // group
    right, left = (c, lax.rem(r + 1, 4)), (c, lax.rem(r + 3, 4))

    barrier = pltpu.get_barrier_semaphore()

    def greet(t, _):
        peer = (lax.rem(c + t, tiles), r)
        pl.semaphore_signal(barrier, inc=1, device_id=peer, device_id_type=MESH)
        return 0

    lax.fori_loop(1, tiles, greet, 0)
    pl.semaphore_signal(barrier, inc=1, device_id=right, device_id_type=MESH)
    pl.semaphore_signal(barrier, inc=1, device_id=left, device_id_type=MESH)

    copy_x = pltpu.make_async_copy(x_any, x, x_sem)
    copy_x.start()

    def fetch_v(t, _):
        pltpu.make_async_copy(
            v_any.at[:, lax.rem(c + t, tiles)], v.at[:, t], v_sem.at[t // group]
        ).start()
        return 0

    lax.fori_loop(0, tiles, fetch_v, 0)

    def fetch_u(t, _):
        pltpu.make_async_copy(u_any.at[:, lax.rem(c + t, tiles)], u.at[:, t], u_sem).start()
        return 0

    lax.fori_loop(0, tiles, fetch_u, 0)
    copy_d = pltpu.make_async_copy(d_any, d, d_sem)
    copy_d.start()

    def rows(q):
        return pl.ds(pl.multiple_of(q * quarter, quarter), quarter)

    def span(g):
        return pl.ds(g * group, group)

    def turned(values, dst):
        for p in range(2):
            hi, lo = halves(values[p].T)
            dst[0, p * s : (p + 1) * s] = hi
            dst[1, p * s : (p + 1) * s] = lo

    def wait_for(ref, sem):
        pltpu.make_async_copy(ref, ref, sem).wait()

    def phase(ph, made_from, lhs, rank_of, spread_by, acc):
        q_right, q_left, q_far = lax.rem(r + 1, 4), lax.rem(r + 3, 4), lax.rem(r + 2, 4)

        def send(src, dst, send_sem, recv_sem, to):
            pltpu.make_async_remote_copy(
                src_ref=src, dst_ref=dst, send_sem=send_sem, recv_sem=recv_sem,
                device_id=to, device_id_type=MESH,
            ).start()

        def produce(g):
            if ph == 0:
                wait_for(v.at[:, span(g)], v_sem.at[g])

            def one(k, _):
                t = g * group + k
                both = jnp.concatenate([made_from[0, t], made_from[1, t]], axis=1)
                y = dot3((lhs[0], lhs[1]), halves(both), ((1,), (0,)))
                kmax = y.shape[1] // 2
                level = lax.broadcasted_iota(jnp.int32, (s, kmax), 1)
                keep = level < rank_of(t)
                part[0, t] = jnp.where(keep, y[:s, :kmax] + y[s:, kmax:], 0.0)
                part[1, t] = jnp.where(keep, y[s:, :kmax] - y[:s, kmax:], 0.0)
                return 0

            lax.fori_loop(0, group, one, 0)

        def rs1(g):
            send(part.at[0, span(g), rows(q_far)], r1.at[ph, 0, span(g)],
                 rs1_send.at[ph, 0], rs1_recv.at[ph, 0, g], right)
            send(part.at[1, span(g), rows(q_far)], r1.at[ph, 1, span(g)],
                 rs1_send.at[ph, 1], rs1_recv.at[ph, 1, g], left)

        def rs2(g):
            for h, q, to in ((0, q_right, right), (1, q_left, left)):
                wait_for(r1.at[ph, h, span(g)], rs1_recv.at[ph, h, g])
                part[h, span(g), rows(q)] = part[h, span(g), rows(q)] + r1[ph, h, span(g)]
                send(part.at[:, span(g), rows(q)], r2.at[ph, h, :, span(g)],
                     rs2_send.at[ph, h], rs2_recv.at[ph, h, g], to)

        def settle(g):
            for h in range(2):
                wait_for(r2.at[ph, h, :, span(g)], rs2_recv.at[ph, h, g])
            for h in range(2):
                part[h, span(g), rows(r)] = part[h, span(g), rows(r)] + (
                    r2[ph, 0, h, span(g)] + r2[ph, 1, h, span(g)]
                )

            def one(k, _):
                t = g * group + k
                src, dst = part.at[:, t, rows(r)], z.at[ph, :, t, rows(r)]

                @pl.when(t == 0)
                def _():
                    pltpu.make_async_copy(src, dst, self_sem.at[ph]).start()

                @pl.when(t > 0)
                def _():
                    send(src, dst, a2a_send.at[ph], a2a_recv.at[ph, g], (lax.rem(c + t, tiles), r))

                return 0

            lax.fori_loop(0, group, one, 0)

        def ag1(g):
            @pl.when(g == 0)
            def _():
                wait_for(z.at[ph, :, 0, rows(r)], self_sem.at[ph])
                if group > 1:
                    wait_for(z.at[ph, :, pl.ds(1, group - 1), rows(r)], a2a_recv.at[ph, 0])

            @pl.when(g > 0)
            def _():
                wait_for(z.at[ph, :, span(g), rows(r)], a2a_recv.at[ph, g])

            own = z.at[ph, :, span(g), rows(r)]
            send(own, own, ag1_send.at[ph, 0], ag1_recv.at[ph, 0, g], right)
            send(own, own, ag1_send.at[ph, 1], ag1_recv.at[ph, 1, g], left)

        def ag2(g):
            for h, q, to in ((0, q_left, right), (1, q_right, left)):
                wait_for(z.at[ph, :, span(g), rows(q)], ag1_recv.at[ph, h, g])
                passed = z.at[ph, h, span(g), rows(q)]
                send(passed, passed, ag2_send.at[ph, h], ag2_recv.at[ph, h, g], to)

        def consume(g):
            for h in range(2):
                wait_for(z.at[ph, h, span(g), rows(q_far)], ag2_recv.at[ph, h, g])

            def one(k, _):
                t = g * group + k
                slot = lax.rem(tiles - t, tiles)
                both = jnp.concatenate([spread_by[0, slot], spread_by[1, slot]], axis=1)
                (ah, al), (bh, bl) = halves(z[ph, 0, t]), halves(z[ph, 1, t])

                def square(a, b):
                    return jnp.concatenate(
                        [jnp.concatenate([a, -b], axis=1), jnp.concatenate([b, a], axis=1)], axis=0
                    )

                acc[...] += dot3(halves(both), (square(ah, bh), square(al, bl)), ((1,), (1,)))
                return 0

            lax.fori_loop(0, group, one, 0)

        def step(it, _):
            def at(lag, f):
                g = it - lag

                @pl.when((g >= 0) & (g < groups))
                def _():
                    f(g)

            at(0, produce)
            at(0, rs1)
            at(lag, ag1)
            at(1, rs2)
            at(2, settle)
            at(lag + 1, ag2)
            if ph == 0:

                @pl.when(it == lag + 2)
                def _():
                    wait_for(u, u_sem)

            at(lag + 2, consume)
            return 0

        lag = max(groups - 2, 3)
        if ph == 0:
            copy_x.wait()
            turned(x, xt)
        acc[...] = jnp.zeros_like(acc)
        if ph == 0:
            pl.semaphore_wait(barrier, tiles + 1)
        lax.fori_loop(0, groups + lag + 2, step, 0)

        for h, q_sum, q_pass in ((0, q_right, q_left), (1, q_left, q_right)):
            wait_for(part.at[h, :, rows(q_far)], rs1_send.at[ph, h])
            wait_for(part.at[:, :, rows(q_sum)], rs2_send.at[ph, h])
            wait_for(z.at[ph, :, :, rows(r)], ag1_send.at[ph, h])
            wait_for(z.at[ph, h, :, rows(q_pass)], ag2_send.at[ph, h])
        wait_for(part.at[:, pl.ds(1, tiles - 1), rows(r)], a2a_send.at[ph])

    phase(0, v, xt, lambda t: ranks[lax.rem(c + t, tiles), c], u, acc_u)
    copy_d.wait()
    for p in range(2):
        d[p] = acc_u[:, p * s : (p + 1) * s] - d[p]
    turned(d, rt)
    copy_res = pltpu.make_async_copy(d, res_any, out_sem.at[0])
    copy_res.start()
    phase(1, u, rt, lambda t: ranks[c, lax.rem(c + t, tiles)], v, acc_v)
    for p in range(2):
        grad[p] = acc_v[:, p * s : (p + 1) * s]
    copy_grad = pltpu.make_async_copy(grad, grad_any, out_sem.at[1])
    copy_grad.start()
    copy_res.wait()
    copy_grad.wait()


def on_device(tiles, group, sources_field, data, left_basis, right_basis, ranks):
    _, n, s = sources_field.shape
    m = data.shape[1]
    k = left_basis.shape[-1]
    groups = tiles // group
    dma = pltpu.SemaphoreType.DMA
    whole = pl.BlockSpec(memory_space=pl.ANY)
    return pl.pallas_call(
        functools.partial(kernel, tiles, group),
        out_shape=(
            jax.ShapeDtypeStruct((2, m, s), F32),
            jax.ShapeDtypeStruct((2, n, s), F32),
        ),
        in_specs=[pl.BlockSpec(memory_space=pltpu.SMEM)] + [whole] * 4,
        out_specs=(whole, whole),
        scratch_shapes=[
            pltpu.VMEM((2, n, s), F32),
            pltpu.VMEM((2, m, s), F32),
            pltpu.VMEM((2, tiles, m, k), F32),
            pltpu.VMEM((2, tiles, n, k), F32),
            pltpu.VMEM((2, tiles, s, k), F32),
            pltpu.VMEM((2, 2, tiles, s // 4, k), F32),
            pltpu.VMEM((2, 2, 2, tiles, s // 4, k), F32),
            pltpu.VMEM((2, 2, tiles, s, k), F32),
            pltpu.VMEM((2, 2 * s, n), BF16),
            pltpu.VMEM((2, 2 * s, m), BF16),
            pltpu.VMEM((m, 2 * s), F32),
            pltpu.VMEM((n, 2 * s), F32),
            pltpu.VMEM((2, n, s), F32),
            dma, dma, dma((groups,)), dma, dma((2,)), dma((2,)),
            dma((2, 2)), dma((2, 2)), dma((2,)), dma((2, 2)), dma((2, 2)),
            dma((2, 2, groups)), dma((2, 2, groups)), dma((2, groups)),
            dma((2, 2, groups)), dma((2, 2, groups)),
        ],
        compiler_params=pltpu.CompilerParams(
            collective_id=0, has_side_effects=True, vmem_limit_bytes=60 * 1024 * 1024
        ),
        name="tlr_step",
    )(ranks, sources_field, data, left_basis, right_basis)


def solution(mesh):
    tiles = mesh.shape["col"]
    group = GROUP if tiles % GROUP == 0 and tiles > 2 * GROUP else 1
    placed = P(None, ("col", "row"), None)
    bases = P(None, None, ("col", "row"), None)
    return jax.shard_map(
        functools.partial(on_device, tiles, group),
        mesh=mesh,
        in_specs=(placed, placed, bases, bases, P()),
        out_specs=(placed, placed),
        check_vma=False,
    )
```

time: 438 us -> 166 us (0.38); the launches traced: 432 us -> 166 us
  waiting for transfers between devices: 238 us -> 0 us
  Pallas kernels: 0 us -> 162 us
  matrix products: 101 us -> 0 us
  blocking collectives: 58.1 us -> 0 us
  between operations: 14.5 us -> 0.64 us
  starting transfers between devices: 7.3 us -> 0 us
  other arithmetic: 5.68 us -> 0 us
    psum x2 -> x0, waiting for transfers between devices: 184 us -> none  [the longest x1 95.7 us: on_device(): summed = lax.psum(partial_coeff, 'row')]
    pallas_call x0 -> x1, Pallas kernels: none -> 162 us  [on_device(): pl.pallas_call(functools.partial(kernel, tiles, group), out_shape=(jax.Sh...]
    dot_general x16 -> x0, matrix products: 101 us -> none  [contract(): jnp.einsum(form, left, right, precision=lax.Precision.HIGHEST, preferred_...]
    all_to_all x1 -> x0, blocking collectives: 58.1 us -> none  [on_device(): lax.all_to_all(back_sum, 'col', split_axis=1, concat_axis=1, tiled=True)]
    all_to_all x1 -> x0, waiting for transfers between devices: 53.8 us -> none  [on_device(): lax.all_to_all(summed, 'col', split_axis=1, concat_axis=1, tiled=True)]
    psum x2 -> x0, local copies, waits for them, and re-layouts: 7.27 us -> none  [the longest x1 4.67 us: on_device(): summed = lax.psum(partial_coeff, 'row')]
    all_to_all x1 -> x0, starting transfers between devices: 7.22 us -> none  [on_device(): lax.all_to_all(summed, 'col', split_axis=1, concat_axis=1, tiled=True)]
    another operation x3 -> x0, other arithmetic: 5.45 us -> none  [the longest x1 2.48 us: on_device(): partial_back = jnp.stack([back_real * keep_left, back_imag * keep_left])]
  transfers between devices with their start and end apart: 3 -> 0, of which waited for: 3 -> 0; matrix products, arithmetic and copies ran while one was open for 0% -> 0% of each run, Pallas kernels for 0% -> 0%
where the time goes in v1:
time: 166 us
  Pallas kernels  162 us (98%)
  local copies, waits for them, and re-layouts  3.44 us (2%)
    pallas_call x1, Pallas kernels, on_device(): pl.pallas_call(functools.partial(kernel, tiles, group), out_shape=(jax.Sh...  162 us
    unnamed x2, local copies, waits for them, and re-layouts  3.44 us

profile of v1, /device:TPU:0, one launch (start us, length us, event | category | flops | bytes accessed | tf_op | source)
XLA Modules:
  0.0 165.8 jit_solution(6673988861900459223)
XLA Ops:
  0.6 161.7 %tlr_step.1 = (f32[2,408,128]{2,1,0:T(8,128)}, f32[2,248,128]{2,1,0:T(8,128)}) custom-call(s32[32,32]{1,0:T(8,128)} %ranks.1, f32[2,248,128]{2,1,0:T(8,128)} %x_any.1, f32[2,408,128]{2,1,0:T(8,128)} %d_any.1, f32[2,32,408,128]{3,2,1,0:T(8,128)} %u_any.1, f32[2,32,248,128]{3,2,1,0:T(8,128)} %v_any.1), custom_call_target="tpu_custom_call" | custom-call | tf_op jit(solution)/shard_map/tlr_step/pallas_call | solution.py:254
  162.3 1.8 %copy.9 = f32[2,408,128]{2,1,0:T(8,128)} copy(f32[2,408,128]{2,1,0:T(8,128)} %get-tuple-element.4) | data formatting | bytes 835584
  164.1 1.7 %copy.10 = f32[2,248,128]{2,1,0:T(8,128)} copy(f32[2,248,128]{2,1,0:T(8,128)} %get-tuple-element.5) | data formatting | bytes 507904

commit v2 on v1

--- a/solution.py
+++ b/solution.py
@@ -11,6 +11,8 @@
 F32 = jnp.float32
 BF16 = jnp.bfloat16
 GROUP = 4
+PACKS = 25
+PACK_GROUP = 5
 
 
 def halves(a):
@@ -26,7 +28,7 @@
     return dot(ah, bh) + (dot(ah, bl) + dot(al, bh))
 
 
-def kernel(
+def plain_kernel(
     tiles, group, ranks, x_any, d_any, u_any, v_any, res_any, grad_any,
     x, d, u, v, part, r1, r2, z, xt, rt, acc_u, acc_v, grad,
     x_sem, d_sem, v_sem, u_sem, out_sem, self_sem,
@@ -244,7 +246,7 @@
     copy_grad.wait()
 
 
-def on_device(tiles, group, sources_field, data, left_basis, right_basis, ranks):
+def plain_step(tiles, group, sources_field, data, left_basis, right_basis, ranks):
     _, n, s = sources_field.shape
     m = data.shape[1]
     k = left_basis.shape[-1]
@@ -252,7 +254,7 @@
     dma = pltpu.SemaphoreType.DMA
     whole = pl.BlockSpec(memory_space=pl.ANY)
     return pl.pallas_call(
-        functools.partial(kernel, tiles, group),
+        functools.partial(plain_kernel, tiles, group),
         out_shape=(
             jax.ShapeDtypeStruct((2, m, s), F32),
             jax.ShapeDtypeStruct((2, n, s), F32),
@@ -281,17 +283,355 @@
         compiler_params=pltpu.CompilerParams(
             collective_id=0, has_side_effects=True, vmem_limit_bytes=60 * 1024 * 1024
         ),
-        name="tlr_step",
+        name="tlr_plain",
     )(ranks, sources_field, data, left_basis, right_basis)
+
+
+def packed_kernel(
+    tiles, packs, group, ranks, x_any, d_any, u_any, v_any, res_any, grad_any,
+    x, d, u, v, ucat, vcat, part, r1, r2, aout, ain00, ain01, ain10, ain11, z, xt, rt, acc_u, acc_v,
+    off, tile_of, x_sem, d_sem, v_sem, u_sem, out_sem, self_sem,
+    rs1_send, rs2_send, a2a_send, ag1_send, ag2_send,
+    rs1_recv, rs2_recv, a2a_recv, ag1_recv, ag2_recv,
+):
+    c = lax.axis_index("col")
+    r = lax.axis_index("row")
+    thick, kmax = part.shape[-2:]
+    level = kmax // 4
+    s = part.shape[0] * 4 * thick
+    groups = packs // group
+    units = 2 * groups
+    right, left = (c, lax.rem(r + 1, 4)), (c, lax.rem(r + 3, 4))
+    q_right, q_left, q_far = lax.rem(r + 1, 4), lax.rem(r + 3, 4), lax.rem(r + 2, 4)
+    ain = ((ain00, ain01), (ain10, ain11))
+
+    def ahead(t):
+        return lax.rem(c + t, tiles)
+
+    def behind(t):
+        return lax.rem(c + tiles - t, tiles)
+
+    barrier = pltpu.get_barrier_semaphore()
+
+    def greet(t, _):
+        pl.semaphore_signal(barrier, inc=1, device_id=(ahead(t), r), device_id_type=MESH)
+        return 0
+
+    copy_x = pltpu.make_async_copy(x_any, x, x_sem)
+    copy_x.start()
+
+    def fetch_v(t, _):
+        pltpu.make_async_copy(v_any.at[:, ahead(t)], v.at[:, t], v_sem).start()
+        return 0
+
+    lax.fori_loop(0, tiles, fetch_v, 0)
+    lax.fori_loop(1, tiles, greet, 0)
+    pl.semaphore_signal(barrier, inc=1, device_id=right, device_id_type=MESH)
+    pl.semaphore_signal(barrier, inc=1, device_id=left, device_id_type=MESH)
+
+    def fetch_u(t, _):
+        pltpu.make_async_copy(u_any.at[:, behind(t)], u.at[:, t], u_sem).start()
+        return 0
+
+    lax.fori_loop(0, tiles, fetch_u, 0)
+    copy_d = pltpu.make_async_copy(d_any, d, d_sem)
+    copy_d.start()
+
+    def tabulate(k, rank_of):
+        off[k, 0] = 0
+
+        def add(t, _):
+            off[k, t + 1] = off[k, t] + rank_of(t) // level
+            return 0
+
+        lax.fori_loop(0, tiles, add, 0)
+
+        def place(b, t):
+            t = jnp.minimum(t + (b >= off[k, t + 1]).astype(jnp.int32), tiles - 1)
+            tile_of[k, b] = t
+            return t
+
+        lax.fori_loop(0, 4 * packs, place, 0)
+
+    def lanes(rows):
+        return lax.broadcasted_iota(jnp.int32, (rows, kmax), 1)
+
+    def packed(k, p, load):
+        out = None
+        for m in range(4):
+            t = tile_of[k, 4 * p + m]
+            run = pltpu.roll(load(t), (off[k, t] & 3) * level, 1)
+            out = run if m == 0 else jnp.where(lanes(run.shape[0]) >= m * level, run, out)
+        return out
+
+    def pack_basis(k, basis, cat, p):
+        for h in range(2):
+            hi, lo = halves(packed(k, p, lambda t: basis[h, t]))
+            cat[0, p, :, h * kmax : (h + 1) * kmax] = hi
+            cat[1, p, :, h * kmax : (h + 1) * kmax] = lo
+
+    def span(g):
+        return pl.ds(g * group, group)
+
+    def turned(values, dst):
+        for p in range(2):
+            hi, lo = halves(values[p].T)
+            dst[0, p * s : (p + 1) * s] = hi
+            dst[1, p * s : (p + 1) * s] = lo
+
+    def wait_for(ref, sem):
+        pltpu.make_async_copy(ref, ref, sem).wait()
+
+    def send(src, dst, send_sem, recv_sem, to):
+        pltpu.make_async_remote_copy(
+            src_ref=src, dst_ref=dst, send_sem=send_sem, recv_sem=recv_sem,
+            device_id=to, device_id_type=MESH,
+        ).start()
+
+    def phase(ph, makes, lhs, made_k, owner_of, spreads, spread_k, acc):
+        def halved(e):
+            return lax.div(e, groups), lax.rem(e, groups)
+
+        def each(g, f):
+            def one(j, _):
+                f(g * group + j)
+                return 0
+
+            lax.fori_loop(0, group, one, 0)
+
+        def produce(g):
+            def one(p):
+                if ph == 0:
+                    pack_basis(0, v, vcat, p)
+                y = dot3((lhs[0], lhs[1]), (makes[0, p], makes[1, p]), ((1,), (0,)))
+                part[:, 0, :, p] = (y[:s, :kmax] + y[s:, kmax:]).reshape(2, 4, thick, kmax)
+                part[:, 1, :, p] = (y[s:, :kmax] - y[:s, kmax:]).reshape(2, 4, thick, kmax)
+
+            each(g, one)
+
+        def rs1(e):
+            f, g = halved(e)
+            send(part.at[f, 0, q_far, span(g)], r1.at[ph, f, 0, span(g)],
+                 rs1_send.at[ph, 0], rs1_recv.at[ph, 0, e], right)
+            send(part.at[f, 1, q_far, span(g)], r1.at[ph, f, 1, span(g)],
+                 rs1_send.at[ph, 1], rs1_recv.at[ph, 1, e], left)
+
+        def rs2(e):
+            f, g = halved(e)
+            for h, q, to in ((0, q_right, right), (1, q_left, left)):
+                wait_for(r1.at[ph, f, h, span(g)], rs1_recv.at[ph, h, e])
+                part[f, h, q, span(g)] = part[f, h, q, span(g)] + r1[ph, f, h, span(g)]
+                send(part.at[f, :, q, span(g)], r2.at[ph, f, h, :, span(g)],
+                     rs2_send.at[ph, h], rs2_recv.at[ph, h, e], to)
+
+        def settle(e):
+            f, g = halved(e)
+            for h in range(2):
+                wait_for(r2.at[ph, f, h, :, span(g)], rs2_recv.at[ph, h, e])
+            for h in range(2):
+                part[f, h, r, span(g)] = part[f, h, r, span(g)] + (
+                    r2[ph, f, 0, h, span(g)] + r2[ph, f, 1, h, span(g)]
+                )
+
+        def deal(f):
+            def unpack(t, _):
+                start = off[made_k, t]
+                p, m = start >> 2, start & 3
+                after = jnp.minimum(p + 1, packs - 1)
+                for h in range(2):
+                    both = jnp.where(
+                        lanes(thick) >= m * level, part[f, h, r, p], part[f, h, r, after]
+                    )
+                    aout[f, t, h] = pltpu.roll(both, ((4 - m) & 3) * level, 1)
+                return 0
+
+            lax.fori_loop(0, tiles, unpack, 0)
+            pltpu.make_async_copy(aout.at[f, 0], ain[ph][f].at[0], self_sem.at[ph, f]).start()
+
+            def one(t, _):
+                send(aout.at[f, t], ain[ph][f].at[t], a2a_send.at[ph],
+                     a2a_recv.at[ph, f], (owner_of(t), r))
+                return 0
+
+            lax.fori_loop(1, tiles, one, 0)
+
+        def gather(f):
+            got = ain[ph][f]
+            wait_for(got.at[0], self_sem.at[ph, f])
+            wait_for(got.at[pl.ds(1, tiles - 1)], a2a_recv.at[ph, f])
+            total = off[spread_k, tiles] * level
+
+            def one(p, _):
+                kept = lanes(thick) + p * kmax < total
+                for h in range(2):
+                    block = packed(spread_k, p, lambda t: got[t, h])
+                    z[ph, f, h, r, p] = jnp.where(kept, block, 0.0)
+                return 0
+
+            lax.fori_loop(0, packs, one, 0)
+
+        def ag1(e):
+            f, g = halved(e)
+            own = z.at[ph, f, :, r, span(g)]
+            send(own, own, ag1_send.at[ph, 0], ag1_recv.at[ph, 0, e], right)
+            send(own, own, ag1_send.at[ph, 1], ag1_recv.at[ph, 1, e], left)
+
+        def ag2(e):
+            f, g = halved(e)
+            for h, q, to in ((0, q_left, right), (1, q_right, left)):
+                wait_for(z.at[ph, f, :, q, span(g)], ag1_recv.at[ph, h, e])
+                passed = z.at[ph, f, h, q, span(g)]
+                send(passed, passed, ag2_send.at[ph, h], ag2_recv.at[ph, h, e], to)
+
+        def consume(g):
+            for f in range(2):
+                for h in range(2):
+                    wait_for(z.at[ph, f, h, q_far, span(g)], ag2_recv.at[ph, h, f * groups + g])
+
+            def one(p):
+                (ah, al), (bh, bl) = (
+                    halves(z[ph, :, h, :, p].reshape(s, kmax)) for h in range(2)
+                )
+
+                def square(a, b):
+                    return jnp.concatenate(
+                        [jnp.concatenate([a, -b], axis=1), jnp.concatenate([b, a], axis=1)], axis=0
+                    )
+
+                acc[...] += dot3(
+                    (spreads[0, p], spreads[1, p]), (square(ah, bh), square(al, bl)), ((1,), (1,))
+                )
+
+            each(g, one)
+
+        lag = groups + 4
+
+        def step(it, _):
+            def at(first, count, f):
+                @pl.when((it >= first) & (it < first + count))
+                def _():
+                    f(it - first)
+
+            at(0, groups, produce)
+            at(0, units, rs1)
+            at(lag, 1, lambda _: gather(0))
+            at(lag + groups, 1, lambda _: gather(1))
+            at(lag, units, ag1)
+            if ph == 0:
+
+                @pl.when(it == groups)
+                def _():
+                    tabulate(1, lambda t: ranks[c, behind(t)])
+                    wait_for(u, u_sem)
+
+                at(groups, groups, lambda g: each(g, functools.partial(pack_basis, 1, u, ucat)))
+            at(1, units, rs2)
+            at(2, units, settle)
+            at(groups + 1, 1, lambda _: deal(0))
+            at(units + 1, 1, lambda _: deal(1))
+            at(lag + 1, units, ag2)
+            at(lag + 2 + groups, groups, consume)
+            return 0
+
+        acc[...] = jnp.zeros_like(acc)
+        if ph == 0:
+            tabulate(0, lambda t: ranks[ahead(t), c])
+            copy_x.wait()
+            turned(x, xt)
+            wait_for(v, v_sem)
+            pl.semaphore_wait(barrier, tiles + 1)
+        lax.fori_loop(0, lag + units + 2, step, 0)
+
+        for h, q_sum, q_pass in ((0, q_right, q_left), (1, q_left, q_right)):
+            wait_for(part.at[:, h, q_far], rs1_send.at[ph, h])
+            wait_for(part.at[:, :, q_sum], rs2_send.at[ph, h])
+            wait_for(z.at[ph, :, :, r], ag1_send.at[ph, h])
+            wait_for(z.at[ph, :, h, q_pass], ag2_send.at[ph, h])
+        wait_for(aout.at[:, pl.ds(1, tiles - 1)], a2a_send.at[ph])
+
+    phase(0, vcat, xt, 0, ahead, ucat, 1, acc_u)
+    copy_d.wait()
+    for p in range(2):
+        d[p] = acc_u[:, p * s : (p + 1) * s] - d[p]
+    turned(d, rt)
+    copy_res = pltpu.make_async_copy(d, res_any, out_sem.at[0])
+    copy_res.start()
+    phase(1, ucat, rt, 1, behind, vcat, 0, acc_v)
+    for p in range(2):
+        x[p] = acc_v[:, p * s : (p + 1) * s]
+    copy_grad = pltpu.make_async_copy(x, grad_any, out_sem.at[1])
+    copy_grad.start()
+    copy_res.wait()
+    copy_grad.wait()
+
+
+def packed_step(tiles, packs, group, collective_id, sources_field, data, left_basis, right_basis, ranks):
+    _, n, s = sources_field.shape
+    m = data.shape[1]
+    k = left_basis.shape[-1]
+    units = 2 * packs // group
+    thick = s // 8
+    dma = pltpu.SemaphoreType.DMA
+    whole = pl.BlockSpec(memory_space=pl.ANY)
+    dealt = pltpu.VMEM((tiles, 2, thick, k), F32)
+    return pl.pallas_call(
+        functools.partial(packed_kernel, tiles, packs, group),
+        out_shape=(
+            jax.ShapeDtypeStruct((2, m, s), F32),
+            jax.ShapeDtypeStruct((2, n, s), F32),
+        ),
+        in_specs=[pl.BlockSpec(memory_space=pltpu.SMEM)] + [whole] * 4,
+        out_specs=(whole, whole),
+        scratch_shapes=[
+            pltpu.VMEM((2, n, s), F32),
+            pltpu.VMEM((2, m, s), F32),
+            pltpu.VMEM((2, tiles, m, k), F32),
+            pltpu.VMEM((2, tiles, n, k), F32),
+            pltpu.VMEM((2, packs, m, 2 * k), BF16),
+            pltpu.VMEM((2, packs, n, 2 * k), BF16),
+            pltpu.VMEM((2, 2, 4, packs, thick, k), F32),
+            pltpu.VMEM((2, 2, 2, packs, thick, k), F32),
+            pltpu.VMEM((2, 2, 2, 2, packs, thick, k), F32),
+            pltpu.VMEM((2, tiles, 2, thick, k), F32),
+            dealt, dealt, dealt, dealt,
+            pltpu.VMEM((2, 2, 2, 4, packs, thick, k), F32),
+            pltpu.VMEM((2, 2 * s, n), BF16),
+            pltpu.VMEM((2, 2 * s, m), BF16),
+            pltpu.VMEM((m, 2 * s), F32),
+            pltpu.VMEM((n, 2 * s), F32),
+            pltpu.SMEM((2, tiles + 1), jnp.int32),
+            pltpu.SMEM((2, 4 * packs), jnp.int32),
+            dma, dma, dma, dma, dma((2,)), dma((2, 2)),
+            dma((2, 2)), dma((2, 2)), dma((2,)), dma((2, 2)), dma((2, 2)),
+            dma((2, 2, units)), dma((2, 2, units)), dma((2, 2)),
+            dma((2, 2, units)), dma((2, 2, units)),
+        ],
+        compiler_params=pltpu.CompilerParams(
+            collective_id=collective_id, has_side_effects=True, vmem_limit_bytes=60 * 1024 * 1024
+        ),
+        name="tlr_packed",
+    )(ranks, sources_field, data, left_basis, right_basis)
+
+
+def on_device(tiles, group, packs, pack_group, *args):
+    runs = args[4] // (args[2].shape[-1] // 4)
+    fits = jnp.maximum(runs.sum(0).max(), runs.sum(1).max()) <= 4 * packs
+    return lax.cond(
+        fits,
+        functools.partial(packed_step, tiles, packs, pack_group, 1),
+        functools.partial(plain_step, tiles, group),
+        *args,
+    )
 
 
 def solution(mesh):
     tiles = mesh.shape["col"]
-    group = GROUP if tiles % GROUP == 0 and tiles > 2 * GROUP else 1
+    wide = tiles % GROUP == 0 and tiles > 2 * GROUP
+    packs, pack_group = (PACKS, PACK_GROUP) if wide else (tiles, 1)
     placed = P(None, ("col", "row"), None)
     bases = P(None, None, ("col", "row"), None)
     return jax.shard_map(
-        functools.partial(on_device, tiles, group),
+        functools.partial(on_device, tiles, GROUP if wide else 1, packs, pack_group),
         mesh=mesh,
         in_specs=(placed, placed, bases, bases, P()),
         out_specs=(placed, placed),

time: 166 us -> 183 us (1.10)
  Pallas kernels: 162 us -> 177 us
  other arithmetic: 0 us -> 2.12 us
  local copies, waits for them, and re-layouts: 3.44 us -> 1.45 us
    pallas_call x1, Pallas kernels: 162 us -> 177 us  [packed_step(): pl.pallas_call(functools.partial(packed_kernel, tiles, packs, group), out...]
    unnamed x2, local copies, waits for them, and re-layouts: 3.44 us -> 1.45 us
where the time goes in v2:
time: 183 us; the launch traced here: 182 us
  Pallas kernels  177 us (97%)
  other arithmetic  2.12 us (1%)
  between operations  1.94 us (1%)
    pallas_call x1, Pallas kernels, packed_step(): pl.pallas_call(functools.partial(packed_kernel, tiles, packs, group), out...  177 us

profile of v2, /device:TPU:0, one launch (start us, length us, event | category | flops | bytes accessed | tf_op | source)
XLA Modules:
  0.0 182.4 jit_solution(2052291947832745576)
XLA Ops:
  0.6 0.9 fusion.2
  1.5 0.6 reduce_max.18
  2.1 0.6 reduce_max.19
  4.0 176.9 %conditional.1 = ((f32[2,408,128]{2,1,0:T(8,128)S(1)}, f32[2,248,128]{2,1,0:T(8,128)S(1)})) conditional(s32[]{:T(128)} %convert_element_type.3, (s32[32,32]{1,0:T(8,128)}, f32[2,248,128]{2,1,0:T(8,128)}, f32[2,408,128]{2,1,0:T(8,128)}, f32[2,32,408,128]{3,2,1,0:T(8,128)}, f32[2,32,248,128]{3,2,1,0:T(8,128)}) %tuple.13, (s32[32,32]{1,0:T(8,128)}, ...), branch_computations={%region_4.5_spmd, %region_5.6_spmd} | conditional | bytes 8 | solution.py:619
  4.1 176.9 %tlr_packed.1 = (f32[2,408,128]{2,1,0:T(8,128)S(1)}, f32[2,248,128]{2,1,0:T(8,128)S(1)}) custom-call(s32[32,32]{1,0:T(8,128)} %get-tuple-element.25.ranks, f32[2,248,128]{2,1,0:T(8,128)} %get-tuple-element.26.x_any, f32[2,408,128]{2,1,0:T(8,128)} %get-tuple-element.27.d_any, f32[2,32,408,128]{3,2,1,0:T(8,128)} %get-tuple-element.28.u_any, ...), custom_call_target="tpu_custom_call" | custom-call | tf_op jit(solution)/shard_map/cond/branch_1_fun/tlr_packed/pallas_call | solution.py:577
  181.0 0.8 copy.17
  181.8 0.7 copy.18

commit v3 on v2

--- a/solution.py
+++ b/solution.py
@@ -13,6 +13,8 @@
 GROUP = 4
 PACKS = 25
 PACK_GROUP = 5
+UNROLL = 4
+STRIDE = 11
 
 
 def halves(a):
@@ -321,7 +323,7 @@
     copy_x.start()
 
     def fetch_v(t, _):
-        pltpu.make_async_copy(v_any.at[:, ahead(t)], v.at[:, t], v_sem).start()
+        pltpu.make_async_copy(v_any.at[:, ahead(t)], v.at[:, t], v_sem.at[t]).start()
         return 0
 
     lax.fori_loop(0, tiles, fetch_v, 0)
@@ -333,9 +335,7 @@
         pltpu.make_async_copy(u_any.at[:, behind(t)], u.at[:, t], u_sem).start()
         return 0
 
-    lax.fori_loop(0, tiles, fetch_u, 0)
     copy_d = pltpu.make_async_copy(d_any, d, d_sem)
-    copy_d.start()
 
     def tabulate(k, rank_of):
         off[k, 0] = 0
@@ -356,13 +356,19 @@
     def lanes(rows):
         return lax.broadcasted_iota(jnp.int32, (rows, kmax), 1)
 
+    def in_place(k, t, run):
+        return pltpu.roll(run, (off[k, t] & 3) * level, 1)
+
     def packed(k, p, load):
         out = None
         for m in range(4):
-            t = tile_of[k, 4 * p + m]
-            run = pltpu.roll(load(t), (off[k, t] & 3) * level, 1)
+            run = load(tile_of[k, 4 * p + m])
             out = run if m == 0 else jnp.where(lanes(run.shape[0]) >= m * level, run, out)
         return out
+
+    def shift_basis(k, basis, t):
+        for h in range(2):
+            basis[h, t] = in_place(k, t, basis[h, t])
 
     def pack_basis(k, basis, cat, p):
         for h in range(2):
@@ -397,7 +403,7 @@
                 f(g * group + j)
                 return 0
 
-            lax.fori_loop(0, group, one, 0)
+            lax.fori_loop(0, group, one, 0, unroll=group)
 
         def produce(g):
             def one(p):
@@ -445,10 +451,11 @@
                     aout[f, t, h] = pltpu.roll(both, ((4 - m) & 3) * level, 1)
                 return 0
 
-            lax.fori_loop(0, tiles, unpack, 0)
+            lax.fori_loop(0, tiles, unpack, 0, unroll=UNROLL)
             pltpu.make_async_copy(aout.at[f, 0], ain[ph][f].at[0], self_sem.at[ph, f]).start()
 
-            def one(t, _):
+            def one(j, _):
+                t = lax.rem(j * STRIDE, tiles)
                 send(aout.at[f, t], ain[ph][f].at[t], a2a_send.at[ph],
                      a2a_recv.at[ph, f], (owner_of(t), r))
                 return 0
@@ -464,11 +471,11 @@
             def one(p, _):
                 kept = lanes(thick) + p * kmax < total
                 for h in range(2):
-                    block = packed(spread_k, p, lambda t: got[t, h])
+                    block = packed(spread_k, p, lambda t: in_place(spread_k, t, got[t, h]))
                     z[ph, f, h, r, p] = jnp.where(kept, block, 0.0)
                 return 0
 
-            lax.fori_loop(0, packs, one, 0)
+            lax.fori_loop(0, packs, one, 0, unroll=group)
 
         def ag1(e):
             f, g = halved(e)
@@ -488,7 +495,9 @@
                 for h in range(2):
                     wait_for(z.at[ph, f, h, q_far, span(g)], ag2_recv.at[ph, h, f * groups + g])
 
-            def one(p):
+            wide, tall = [], []
+            for j in range(group):
+                p = g * group + j
                 (ah, al), (bh, bl) = (
                     halves(z[ph, :, h, :, p].reshape(s, kmax)) for h in range(2)
                 )
@@ -498,39 +507,52 @@
                         [jnp.concatenate([a, -b], axis=1), jnp.concatenate([b, a], axis=1)], axis=0
                     )
 
-                acc[...] += dot3(
-                    (spreads[0, p], spreads[1, p]), (square(ah, bh), square(al, bl)), ((1,), (1,))
-                )
-
-            each(g, one)
-
-        lag = groups + 4
+                high, low = square(ah, bh), square(al, bl)
+                wide += [spreads[0, p], spreads[0, p], spreads[1, p]]
+                tall += [high, low, high]
+            acc[...] += lax.dot_general(
+                jnp.concatenate(wide, axis=1), jnp.concatenate(tall, axis=1),
+                (((1,), (1,)), ((), ())), preferred_element_type=F32,
+            )
+
+        sum1, sum2, own = (1, groups + 2), (3, groups + 3), (groups + 7, 2 * groups + 7)
+        passes, last = (own[0] + 2, own[1] + 2), own[1] + 3
+        chunk = -(-tiles // 4)
 
         def step(it, _):
-            def at(first, count, f):
+            def at(first, count, f, base=0):
                 @pl.when((it >= first) & (it < first + count))
                 def _():
-                    f(it - first)
+                    f(it - first + base)
+
+            def both(first, f):
+                at(first[0], groups, f)
+                at(first[1], groups, f, groups)
 
             at(0, groups, produce)
             at(0, units, rs1)
-            at(lag, 1, lambda _: gather(0))
-            at(lag + groups, 1, lambda _: gather(1))
-            at(lag, units, ag1)
+            at(own[0], 1, lambda _: gather(0))
+            at(own[1], 1, lambda _: gather(1))
+            both(own, ag1)
+            both(sum1, rs2)
+            both(passes, ag2)
             if ph == 0:
-
-                @pl.when(it == groups)
-                def _():
-                    tabulate(1, lambda t: ranks[c, behind(t)])
-                    wait_for(u, u_sem)
-
-                at(groups, groups, lambda g: each(g, functools.partial(pack_basis, 1, u, ucat)))
-            at(1, units, rs2)
-            at(2, units, settle)
-            at(groups + 1, 1, lambda _: deal(0))
-            at(units + 1, 1, lambda _: deal(1))
-            at(lag + 1, units, ag2)
-            at(lag + 2 + groups, groups, consume)
+                at(groups, 1, lambda _: tabulate(1, lambda t: ranks[c, behind(t)]))
+                at(groups, 1, lambda _: wait_for(u, u_sem))
+
+                def shift(j):
+                    def one(t, _):
+                        shift_basis(1, u, t)
+                        return 0
+
+                    lax.fori_loop(j * chunk, jnp.minimum((j + 1) * chunk, tiles), one, 0)
+
+                at(groups, 4, shift)
+                at(groups + 4, groups, lambda g: each(g, functools.partial(pack_basis, 1, u, ucat)))
+            both(sum2, settle)
+            at(sum2[0] + groups - 1, 1, lambda _: deal(0))
+            at(sum2[1] + groups - 1, 1, lambda _: deal(1))
+            at(last, groups, consume)
             return 0
 
         acc[...] = jnp.zeros_like(acc)
@@ -538,9 +560,17 @@
             tabulate(0, lambda t: ranks[ahead(t), c])
             copy_x.wait()
             turned(x, xt)
-            wait_for(v, v_sem)
+
+            def settle_v(t, _):
+                wait_for(v.at[:, t], v_sem.at[t])
+                shift_basis(0, v, t)
+                return 0
+
+            lax.fori_loop(0, tiles, settle_v, 0)
+            lax.fori_loop(0, tiles, fetch_u, 0)
+            copy_d.start()
             pl.semaphore_wait(barrier, tiles + 1)
-        lax.fori_loop(0, lag + units + 2, step, 0)
+        lax.fori_loop(0, last + groups, step, 0)
 
         for h, q_sum, q_pass in ((0, q_right, q_left), (1, q_left, q_right)):
             wait_for(part.at[:, h, q_far], rs1_send.at[ph, h])
@@ -601,7 +631,7 @@
             pltpu.VMEM((n, 2 * s), F32),
             pltpu.SMEM((2, tiles + 1), jnp.int32),
             pltpu.SMEM((2, 4 * packs), jnp.int32),
-            dma, dma, dma, dma, dma((2,)), dma((2, 2)),
+            dma, dma, dma((tiles,)), dma, dma((2,)), dma((2, 2)),
             dma((2, 2)), dma((2, 2)), dma((2,)), dma((2, 2)), dma((2, 2)),
             dma((2, 2, units)), dma((2, 2, units)), dma((2, 2)),
             dma((2, 2, units)), dma((2, 2, units)),

time: 183 us -> 153 us (0.84)
  Pallas kernels: 177 us -> 148 us
    pallas_call x1, Pallas kernels: 177 us -> 148 us  [packed_step(): pl.pallas_call(functools.partial(packed_kernel, tiles, packs, group), out...]
where the time goes in v3:
time: 153 us
  Pallas kernels  148 us (97%)
  other arithmetic  2.12 us (1%)
  between operations  1.94 us (1%)
    pallas_call x1, Pallas kernels, packed_step(): pl.pallas_call(functools.partial(packed_kernel, tiles, packs, group), out...  148 us

profile of v3, /device:TPU:0, one launch (start us, length us, event | category | flops | bytes accessed | tf_op | source)
XLA Modules:
  0.0 153.1 jit_solution(10624025966224143869)
XLA Ops:
  0.6 0.9 fusion.2
  1.5 0.6 reduce_max.18
  2.1 0.6 reduce_max.19
  4.0 147.6 %conditional.1 = ((f32[2,408,128]{2,1,0:T(8,128)S(1)}, f32[2,248,128]{2,1,0:T(8,128)S(1)})) conditional(s32[]{:T(128)} %convert_element_type.3, (s32[32,32]{1,0:T(8,128)}, f32[2,248,128]{2,1,0:T(8,128)}, f32[2,408,128]{2,1,0:T(8,128)}, f32[2,32,408,128]{3,2,1,0:T(8,128)}, f32[2,32,248,128]{3,2,1,0:T(8,128)}) %tuple.13, (s32[32,32]{1,0:T(8,128)}, ...), branch_computations={%region_4.5_spmd, %region_5.6_spmd} | conditional | bytes 8 | solution.py:649
  4.1 147.6 %tlr_packed.1 = (f32[2,408,128]{2,1,0:T(8,128)S(1)}, f32[2,248,128]{2,1,0:T(8,128)S(1)}) custom-call(s32[32,32]{1,0:T(8,128)} %get-tuple-element.25.ranks, f32[2,248,128]{2,1,0:T(8,128)} %get-tuple-element.26.x_any, f32[2,408,128]{2,1,0:T(8,128)} %get-tuple-element.27.d_any, f32[2,32,408,128]{3,2,1,0:T(8,128)} %get-tuple-element.28.u_any, ...), custom_call_target="tpu_custom_call" | custom-call | tf_op jit(solution)/shard_map/cond/branch_1_fun/tlr_packed/pallas_call | solution.py:607
  151.7 0.8 copy.17
  152.4 0.7 copy.18

commit v4 on v3

--- a/solution.py
+++ b/solution.py
@@ -1,4 +1,5 @@
 import functools
+import types
 
 import jax
 import jax.numpy as jnp
@@ -379,12 +380,6 @@
     def span(g):
         return pl.ds(g * group, group)
 
-    def turned(values, dst):
-        for p in range(2):
-            hi, lo = halves(values[p].T)
-            dst[0, p * s : (p + 1) * s] = hi
-            dst[1, p * s : (p + 1) * s] = lo
-
     def wait_for(ref, sem):
         pltpu.make_async_copy(ref, ref, sem).wait()
 
@@ -394,7 +389,7 @@
             device_id=to, device_id_type=MESH,
         ).start()
 
-    def phase(ph, makes, lhs, made_k, owner_of, spreads, spread_k, acc):
+    def phase(ph, makes, made_k, owner_of, spreads, spread_k):
         def halved(e):
             return lax.div(e, groups), lax.rem(e, groups)
 
@@ -407,20 +402,42 @@
 
         def produce(g):
             def one(p):
-                if ph == 0:
-                    pack_basis(0, v, vcat, p)
-                y = dot3((lhs[0], lhs[1]), (makes[0, p], makes[1, p]), ((1,), (0,)))
+                pack_basis(0, v, vcat, p)
+                y = dot3((xt[0], xt[1]), (makes[0, p], makes[1, p]), ((1,), (0,)))
                 part[:, 0, :, p] = (y[:s, :kmax] + y[s:, kmax:]).reshape(2, 4, thick, kmax)
                 part[:, 1, :, p] = (y[s:, :kmax] - y[:s, kmax:]).reshape(2, 4, thick, kmax)
 
             each(g, one)
+
+        def produce_half(f, g):
+            n = s // 2
+
+            def one(p):
+                y = dot3((rt[f, 0], rt[f, 1]), (makes[0, p], makes[1, p]), ((1,), (0,)))
+                part[f, 0, :, p] = (y[:n, :kmax] + y[n:, kmax:]).reshape(4, thick, kmax)
+                part[f, 1, :, p] = (y[n:, :kmax] - y[:n, kmax:]).reshape(4, thick, kmax)
+
+            each(g, one)
+
+        def sums_sent(f):
+            for h, q in ((0, q_right), (1, q_left)):
+                wait_for(part.at[f, h, q_far], rs1_send.at[ph, f, h])
+                wait_for(part.at[f, :, q], rs2_send.at[ph, f, h])
+
+        def dealt(f):
+            wait_for(aout.at[f, pl.ds(1, tiles - 1)], a2a_send.at[ph, f])
+
+        def gathered():
+            for h, q in ((0, q_left), (1, q_right)):
+                wait_for(z.at[ph, :, :, r], ag1_send.at[ph, h])
+                wait_for(z.at[ph, :, h, q], ag2_send.at[ph, h])
 
         def rs1(e):
             f, g = halved(e)
             send(part.at[f, 0, q_far, span(g)], r1.at[ph, f, 0, span(g)],
-                 rs1_send.at[ph, 0], rs1_recv.at[ph, 0, e], right)
+                 rs1_send.at[ph, f, 0], rs1_recv.at[ph, 0, e], right)
             send(part.at[f, 1, q_far, span(g)], r1.at[ph, f, 1, span(g)],
-                 rs1_send.at[ph, 1], rs1_recv.at[ph, 1, e], left)
+                 rs1_send.at[ph, f, 1], rs1_recv.at[ph, 1, e], left)
 
         def rs2(e):
             f, g = halved(e)
@@ -428,7 +445,7 @@
                 wait_for(r1.at[ph, f, h, span(g)], rs1_recv.at[ph, h, e])
                 part[f, h, q, span(g)] = part[f, h, q, span(g)] + r1[ph, f, h, span(g)]
                 send(part.at[f, :, q, span(g)], r2.at[ph, f, h, :, span(g)],
-                     rs2_send.at[ph, h], rs2_recv.at[ph, h, e], to)
+                     rs2_send.at[ph, f, h], rs2_recv.at[ph, h, e], to)
 
         def settle(e):
             f, g = halved(e)
@@ -456,7 +473,7 @@
 
             def one(j, _):
                 t = lax.rem(j * STRIDE, tiles)
-                send(aout.at[f, t], ain[ph][f].at[t], a2a_send.at[ph],
+                send(aout.at[f, t], ain[ph][f].at[t], a2a_send.at[ph, f],
                      a2a_recv.at[ph, f], (owner_of(t), r))
                 return 0
 
@@ -490,17 +507,15 @@
                 passed = z.at[ph, f, h, q, span(g)]
                 send(passed, passed, ag2_send.at[ph, h], ag2_recv.at[ph, h, e], to)
 
-        def consume(g):
-            for f in range(2):
-                for h in range(2):
-                    wait_for(z.at[ph, f, h, q_far, span(g)], ag2_recv.at[ph, h, f * groups + g])
-
+        def arrived(f, g):
+            for h in range(2):
+                wait_for(z.at[ph, f, h, q_far, span(g)], ag2_recv.at[ph, h, f * groups + g])
+
+        def spread(g, coeffs):
             wide, tall = [], []
             for j in range(group):
                 p = g * group + j
-                (ah, al), (bh, bl) = (
-                    halves(z[ph, :, h, :, p].reshape(s, kmax)) for h in range(2)
-                )
+                (ah, al), (bh, bl) = (halves(coeffs(h, p)) for h in range(2))
 
                 def square(a, b):
                     return jnp.concatenate(
@@ -510,87 +525,130 @@
                 high, low = square(ah, bh), square(al, bl)
                 wide += [spreads[0, p], spreads[0, p], spreads[1, p]]
                 tall += [high, low, high]
-            acc[...] += lax.dot_general(
+            return lax.dot_general(
                 jnp.concatenate(wide, axis=1), jnp.concatenate(tall, axis=1),
                 (((1,), (1,)), ((), ())), preferred_element_type=F32,
             )
 
-        sum1, sum2, own = (1, groups + 2), (3, groups + 3), (groups + 7, 2 * groups + 7)
-        passes, last = (own[0] + 2, own[1] + 2), own[1] + 3
-        chunk = -(-tiles // 4)
-
-        def step(it, _):
-            def at(first, count, f, base=0):
-                @pl.when((it >= first) & (it < first + count))
-                def _():
-                    f(it - first + base)
-
-            def both(first, f):
-                at(first[0], groups, f)
-                at(first[1], groups, f, groups)
-
-            at(0, groups, produce)
-            at(0, units, rs1)
-            at(own[0], 1, lambda _: gather(0))
-            at(own[1], 1, lambda _: gather(1))
-            both(own, ag1)
-            both(sum1, rs2)
-            both(passes, ag2)
-            if ph == 0:
-                at(groups, 1, lambda _: tabulate(1, lambda t: ranks[c, behind(t)]))
-                at(groups, 1, lambda _: wait_for(u, u_sem))
-
-                def shift(j):
-                    def one(t, _):
-                        shift_basis(1, u, t)
-                        return 0
-
-                    lax.fori_loop(j * chunk, jnp.minimum((j + 1) * chunk, tiles), one, 0)
-
-                at(groups, 4, shift)
-                at(groups + 4, groups, lambda g: each(g, functools.partial(pack_basis, 1, u, ucat)))
-            both(sum2, settle)
-            at(sum2[0] + groups - 1, 1, lambda _: deal(0))
-            at(sum2[1] + groups - 1, 1, lambda _: deal(1))
-            at(last, groups, consume)
-            return 0
-
-        acc[...] = jnp.zeros_like(acc)
-        if ph == 0:
-            tabulate(0, lambda t: ranks[ahead(t), c])
-            copy_x.wait()
-            turned(x, xt)
-
-            def settle_v(t, _):
-                wait_for(v.at[:, t], v_sem.at[t])
-                shift_basis(0, v, t)
+        def consume(g):
+            for f in range(2):
+                arrived(f, g)
+            acc_v[...] += spread(g, lambda h, p: z[ph, :, h, :, p].reshape(s, kmax))
+
+        def consume_half(f, g):
+            arrived(f, g)
+            acc_u[f] += spread(g, lambda h, p: z[ph, f, h, :, p].reshape(s // 2, kmax))
+
+        return types.SimpleNamespace(**locals())
+
+    fwd = phase(0, vcat, 0, ahead, ucat, 1)
+    adj = phase(1, ucat, 1, behind, vcat, 0)
+
+    def subtract(f):
+        n = s // 2
+        given = jnp.concatenate([d[h, :, f * n : (f + 1) * n] for h in range(2)], axis=1)
+        rest = acc_u[f] - given
+        hi, lo = halves(rest.T)
+        rt[f, 0] = hi
+        rt[f, 1] = lo
+        for h in range(2):
+            d[h, :, f * n : (f + 1) * n] = rest[:, h * n : (h + 1) * n]
+
+    sum1, sum2, own = (2, groups + 2), (4, groups + 4), (groups + 7, 2 * groups + 7)
+    passes, used = (own[0] + 2, own[1] + 2), (own[0] + 4, own[1] + 4)
+    second = used[0] + groups
+    chunk = -(-tiles // 4)
+
+    def step(it, _):
+        def at(first, count, f, base=0):
+            @pl.when((it >= first) & (it < first + count))
+            def _():
+                f(it - first + base)
+
+        def both(first, f):
+            at(first[0], groups, f)
+            at(first[1], groups, f, groups)
+
+        def once(when, f, *given):
+            at(when, 1, lambda _: f(*given))
+
+        def later(pair):
+            return tuple(first + second for first in pair)
+
+        at(0, groups, fwd.produce)
+        at(0, units, fwd.rs1)
+        once(own[0], fwd.gather, 0)
+        once(own[1], fwd.gather, 1)
+        both(own, fwd.ag1)
+        both(sum1, fwd.rs2)
+        both(passes, fwd.ag2)
+        once(groups, tabulate, 1, lambda t: ranks[c, behind(t)])
+        once(groups, wait_for, u, u_sem)
+
+        def shift(j):
+            def one(t, _):
+                shift_basis(1, u, t)
                 return 0
 
-            lax.fori_loop(0, tiles, settle_v, 0)
-            lax.fori_loop(0, tiles, fetch_u, 0)
-            copy_d.start()
-            pl.semaphore_wait(barrier, tiles + 1)
-        lax.fori_loop(0, last + groups, step, 0)
-
-        for h, q_sum, q_pass in ((0, q_right, q_left), (1, q_left, q_right)):
-            wait_for(part.at[:, h, q_far], rs1_send.at[ph, h])
-            wait_for(part.at[:, :, q_sum], rs2_send.at[ph, h])
-            wait_for(z.at[ph, :, :, r], ag1_send.at[ph, h])
-            wait_for(z.at[ph, :, h, q_pass], ag2_send.at[ph, h])
-        wait_for(aout.at[:, pl.ds(1, tiles - 1)], a2a_send.at[ph])
-
-    phase(0, vcat, xt, 0, ahead, ucat, 1, acc_u)
-    copy_d.wait()
+            lax.fori_loop(j * chunk, jnp.minimum((j + 1) * chunk, tiles), one, 0)
+
+        at(groups, 4, shift)
+        at(groups + 4, groups, lambda g: fwd.each(g, functools.partial(pack_basis, 1, u, ucat)))
+        both(sum2, fwd.settle)
+        for f in range(2):
+            once(sum2[f] + groups - 1, fwd.deal, f)
+        once(used[0], copy_d.wait)
+        for f in range(2):
+            at(used[f], groups, functools.partial(fwd.consume_half, f))
+            once(used[f] + groups - 1, subtract, f)
+
+        for f in range(2):
+            once(second + f * groups, fwd.sums_sent, f)
+            at(second + f * groups, groups, functools.partial(adj.produce_half, f))
+        at(second, units, adj.rs1)
+        once(second + own[0], adj.gather, 0)
+        once(second + own[1], adj.gather, 1)
+        both(later(own), adj.ag1)
+        both(later(sum1), adj.rs2)
+        both(later(passes), adj.ag2)
+        both(later(sum2), adj.settle)
+        for f in range(2):
+            once(second + sum2[f] + groups - 1, fwd.dealt, f)
+            once(second + sum2[f] + groups - 1, adj.deal, f)
+        once(second + 2 * groups, lambda: copy_res.start())
+        at(second + used[1], groups, adj.consume)
+        return 0
+
+    copy_res = pltpu.make_async_copy(d, res_any, out_sem.at[0])
+    acc_u[...] = jnp.zeros_like(acc_u)
+    acc_v[...] = jnp.zeros_like(acc_v)
+    tabulate(0, lambda t: ranks[ahead(t), c])
+    copy_x.wait()
     for p in range(2):
-        d[p] = acc_u[:, p * s : (p + 1) * s] - d[p]
-    turned(d, rt)
-    copy_res = pltpu.make_async_copy(d, res_any, out_sem.at[0])
-    copy_res.start()
-    phase(1, ucat, rt, 1, behind, vcat, 0, acc_v)
+        hi, lo = halves(x[p].T)
+        xt[0, p * s : (p + 1) * s] = hi
+        xt[1, p * s : (p + 1) * s] = lo
+
+    def settle_v(t, _):
+        wait_for(v.at[:, t], v_sem.at[t])
+        shift_basis(0, v, t)
+        return 0
+
+    lax.fori_loop(0, tiles, settle_v, 0)
+    lax.fori_loop(0, tiles, fetch_u, 0)
+    copy_d.start()
+    pl.semaphore_wait(barrier, tiles + 1)
+    lax.fori_loop(0, second + used[1] + groups, step, 0)
+
     for p in range(2):
         x[p] = acc_v[:, p * s : (p + 1) * s]
     copy_grad = pltpu.make_async_copy(x, grad_any, out_sem.at[1])
     copy_grad.start()
+    fwd.gathered()
+    adj.gathered()
+    for f in range(2):
+        adj.sums_sent(f)
+        adj.dealt(f)
     copy_res.wait()
     copy_grad.wait()
 
@@ -626,13 +684,13 @@
             dealt, dealt, dealt, dealt,
             pltpu.VMEM((2, 2, 2, 4, packs, thick, k), F32),
             pltpu.VMEM((2, 2 * s, n), BF16),
-            pltpu.VMEM((2, 2 * s, m), BF16),
-            pltpu.VMEM((m, 2 * s), F32),
+            pltpu.VMEM((2, 2, s, m), BF16),
+            pltpu.VMEM((2, m, s), F32),
             pltpu.VMEM((n, 2 * s), F32),
             pltpu.SMEM((2, tiles + 1), jnp.int32),
             pltpu.SMEM((2, 4 * packs), jnp.int32),
             dma, dma, dma((tiles,)), dma, dma((2,)), dma((2, 2)),
-            dma((2, 2)), dma((2, 2)), dma((2,)), dma((2, 2)), dma((2, 2)),
+            dma((2, 2, 2)), dma((2, 2, 2)), dma((2, 2)), dma((2, 2)), dma((2, 2)),
             dma((2, 2, units)), dma((2, 2, units)), dma((2, 2)),
             dma((2, 2, units)), dma((2, 2, units)),
         ],

time: 153 us -> 136 us (0.89)
  Pallas kernels: 148 us -> 130 us
    pallas_call x1, Pallas kernels: 148 us -> 130 us  [packed_step(): pl.pallas_call(functools.partial(packed_kernel, tiles, packs, group), out...]
where the time goes in v4:
time: 136 us
  Pallas kernels  130 us (96%)
  other arithmetic  2.12 us (2%)
  between operations  1.94 us (1%)
  local copies, waits for them, and re-layouts  1.45 us (1%)
    pallas_call x1, Pallas kernels, packed_step(): pl.pallas_call(functools.partial(packed_kernel, tiles, packs, group), out...  130 us

profile of v4, /device:TPU:0, one launch (start us, length us, event | category | flops | bytes accessed | tf_op | source)
XLA Modules:
  0.0 135.9 jit_solution(9483210309256373487)
XLA Ops:
  0.6 0.9 fusion.2
  1.5 0.6 reduce_max.18
  2.1 0.6 reduce_max.19
  4.0 130.3 %conditional.1 = ((f32[2,408,128]{2,1,0:T(8,128)S(1)}, f32[2,248,128]{2,1,0:T(8,128)S(1)})) conditional(s32[]{:T(128)} %convert_element_type.3, (s32[32,32]{1,0:T(8,128)}, f32[2,248,128]{2,1,0:T(8,128)}, f32[2,408,128]{2,1,0:T(8,128)}, f32[2,32,408,128]{3,2,1,0:T(8,128)}, f32[2,32,248,128]{3,2,1,0:T(8,128)}) %tuple.13, (s32[32,32]{1,0:T(8,128)}, ...), branch_computations={%region_4.5_spmd, %region_5.6_spmd} | conditional | bytes 8 | solution.py:707
  4.1 130.3 %tlr_packed.1 = (f32[2,408,128]{2,1,0:T(8,128)S(1)}, f32[2,248,128]{2,1,0:T(8,128)S(1)}) custom-call(s32[32,32]{1,0:T(8,128)} %get-tuple-element.25.ranks, f32[2,248,128]{2,1,0:T(8,128)} %get-tuple-element.26.x_any, f32[2,408,128]{2,1,0:T(8,128)} %get-tuple-element.27.d_any, f32[2,32,408,128]{3,2,1,0:T(8,128)} %get-tuple-element.28.u_any, ...), custom_call_target="tpu_custom_call" | custom-call | tf_op jit(solution)/shard_map/cond/branch_1_fun/tlr_packed/pallas_call | solution.py:665
  134.4 0.8 copy.17
  135.2 0.7 copy.18

commit v5 on v4

--- a/solution.py
+++ b/solution.py
@@ -12,8 +12,7 @@
 F32 = jnp.float32
 BF16 = jnp.bfloat16
 GROUP = 4
-PACKS = 25
-PACK_GROUP = 5
+SIZES = ((24, 6), (25, 5))
 UNROLL = 4
 STRIDE = 11
 
@@ -631,10 +630,15 @@
 
     def settle_v(t, _):
         wait_for(v.at[:, t], v_sem.at[t])
+        return 0
+
+    lax.fori_loop(0, tiles, settle_v, 0)
+
+    def shift_v(t, _):
         shift_basis(0, v, t)
         return 0
 
-    lax.fori_loop(0, tiles, settle_v, 0)
+    lax.fori_loop(0, tiles, shift_v, 0, unroll=UNROLL)
     lax.fori_loop(0, tiles, fetch_u, 0)
     copy_d.start()
     pl.semaphore_wait(barrier, tiles + 1)
@@ -701,25 +705,25 @@
     )(ranks, sources_field, data, left_basis, right_basis)
 
 
-def on_device(tiles, group, packs, pack_group, *args):
+def on_device(tiles, group, sizes, *args):
     runs = args[4] // (args[2].shape[-1] // 4)
-    fits = jnp.maximum(runs.sum(0).max(), runs.sum(1).max()) <= 4 * packs
-    return lax.cond(
-        fits,
-        functools.partial(packed_step, tiles, packs, pack_group, 1),
-        functools.partial(plain_step, tiles, group),
-        *args,
-    )
+    most = jnp.stack([runs, runs.T]).sum(1).max()
+    choice = sum((most > 4 * packs).astype(jnp.int32) for packs, _ in sizes)
+    forms = [
+        functools.partial(packed_step, tiles, packs, pack_group, 1 + i)
+        for i, (packs, pack_group) in enumerate(sizes)
+    ]
+    return lax.switch(choice, forms + [functools.partial(plain_step, tiles, group)], *args)
 
 
 def solution(mesh):
     tiles = mesh.shape["col"]
     wide = tiles % GROUP == 0 and tiles > 2 * GROUP
-    packs, pack_group = (PACKS, PACK_GROUP) if wide else (tiles, 1)
+    sizes = SIZES if wide else ((tiles, 1),)
     placed = P(None, ("col", "row"), None)
     bases = P(None, None, ("col", "row"), None)
     return jax.shard_map(
-        functools.partial(on_device, tiles, GROUP if wide else 1, packs, pack_group),
+        functools.partial(on_device, tiles, GROUP if wide else 1, sizes),
         mesh=mesh,
         in_specs=(placed, placed, bases, bases, P()),
         out_specs=(placed, placed),

time: 136 us -> 133 us (0.978)
  Pallas kernels: 130 us -> 128 us
  other arithmetic: 2.12 us -> 0.68 us
    pallas_call x1, Pallas kernels: 130 us -> 128 us  [packed_step(): pl.pallas_call(functools.partial(packed_kernel, tiles, packs, group), out...]
where the time goes in v5:
time: 133 us
  Pallas kernels  128 us (96%)
  local copies, waits for them, and re-layouts  2.31 us (2%)
  between operations  1.95 us (1%)
    pallas_call x1, Pallas kernels, packed_step(): pl.pallas_call(functools.partial(packed_kernel, tiles, packs, group), out...  128 us

profile of v5, /device:TPU:0, one launch (start us, length us, event | category | flops | bytes accessed | tf_op | source)
XLA Modules:
  0.0 132.9 jit_solution(18292615519061504879)
XLA Ops:
  0.6 0.8 copy.18
  1.4 0.1 copy.22
  1.5 0.6 reduce_max.9
  3.5 127.9 %conditional.1 = ((f32[2,408,128]{2,1,0:T(8,128)S(1)}, f32[2,248,128]{2,1,0:T(8,128)S(1)})) conditional(s32[]{:T(128)} %clamp.3, (s32[32,32]{1,0:T(8,128)}, f32[2,248,128]{2,1,0:T(8,128)}, f32[2,408,128]{2,1,0:T(8,128)}, f32[2,32,408,128]{3,2,1,0:T(8,128)}, f32[2,32,248,128]{3,2,1,0:T(8,128)}) %tuple.16, (s32[32,32]{1,0:T(8,128)}, ...), branch_computations={%region_2.3_spmd, %region_3.4_spmd, %region_4.5_spmd} | conditional | bytes 8 | solution.py:716
  3.5 127.7 %tlr_packed.2 = (f32[2,408,128]{2,1,0:T(8,128)S(1)}, f32[2,248,128]{2,1,0:T(8,128)S(1)}) custom-call(s32[32,32]{1,0:T(8,128)} %get-tuple-element.30.ranks, f32[2,248,128]{2,1,0:T(8,128)} %get-tuple-element.31.x_any, f32[2,408,128]{2,1,0:T(8,128)} %get-tuple-element.32.d_any, f32[2,32,408,128]{3,2,1,0:T(8,128)} %get-tuple-element.33.u_any, ...), custom_call_target="tpu_custom_call" | custom-call | tf_op jit(solution)/shard_map/cond/branch_0_fun/tlr_packed/pallas_call | solution.py:669
  131.4 0.8 copy.31
  132.2 0.7 copy.32
  (2 shorter events, 0.0 us)

commit v6 on v5

--- a/solution.py
+++ b/solution.py
@@ -13,7 +13,7 @@
 BF16 = jnp.bfloat16
 GROUP = 4
 SIZES = ((24, 6), (25, 5))
-UNROLL = 4
+UNROLL = 8
 STRIDE = 11
 
 

time: 133 us -> 132 us (level)
  no operation moved by 1% of the time
where the time goes in v6:
time: 132 us
  Pallas kernels  127 us (96%)
  local copies, waits for them, and re-layouts  2.31 us (2%)
  between operations  1.95 us (1%)
    pallas_call x1, Pallas kernels, packed_step(): pl.pallas_call(functools.partial(packed_kernel, tiles, packs, group), out...  127 us

profile of v6, /device:TPU:0, one launch (start us, length us, event | category | flops | bytes accessed | tf_op | source)
XLA Modules:
  0.0 132.2 jit_solution(13988625070668035602)
XLA Ops:
  0.6 0.8 copy.18
  1.4 0.1 copy.22
  1.5 0.6 reduce_max.9
  3.5 127.2 %conditional.1 = ((f32[2,408,128]{2,1,0:T(8,128)S(1)}, f32[2,248,128]{2,1,0:T(8,128)S(1)})) conditional(s32[]{:T(128)} %clamp.3, (s32[32,32]{1,0:T(8,128)}, f32[2,248,128]{2,1,0:T(8,128)}, f32[2,408,128]{2,1,0:T(8,128)}, f32[2,32,408,128]{3,2,1,0:T(8,128)}, f32[2,32,248,128]{3,2,1,0:T(8,128)}) %tuple.16, (s32[32,32]{1,0:T(8,128)}, ...), branch_computations={%region_2.3_spmd, %region_3.4_spmd, %region_4.5_spmd} | conditional | bytes 8 | solution.py:716
  3.5 127.0 %tlr_packed.2 = (f32[2,408,128]{2,1,0:T(8,128)S(1)}, f32[2,248,128]{2,1,0:T(8,128)S(1)}) custom-call(s32[32,32]{1,0:T(8,128)} %get-tuple-element.30.ranks, f32[2,248,128]{2,1,0:T(8,128)} %get-tuple-element.31.x_any, f32[2,408,128]{2,1,0:T(8,128)} %get-tuple-element.32.d_any, f32[2,32,408,128]{3,2,1,0:T(8,128)} %get-tuple-element.33.u_any, ...), custom_call_target="tpu_custom_call" | custom-call | tf_op jit(solution)/shard_map/cond/branch_0_fun/tlr_packed/pallas_call | solution.py:669
  130.7 0.8 copy.31
  131.5 0.7 copy.32
  (2 shorter events, 0.0 us)
